TPU v7x, 512 devices: a whole 4x8x8 slice. The times are simulated.
512 devices in a mesh: grp: 16 (over z, core), sp: 32 (over x, y).
Axes of the slice: x: 4, y: 8, z: 8, core: 2. Of those that a mesh axis runs over, the one named last changes fastest.
Arguments:
- query_input: bfloat16 [65536, 4096], P(('grp', 'sp')), may hold values from -6 to 6
- key_input: bfloat16 [65536, 4096], P(('grp', 'sp')), may hold values from -6 to 6
- value_heads_input: bfloat16 [65536, 4096], P(('grp', 'sp')), may hold values from -6 to 6
- conv_weight: float32 [3, 4, 4096], P(None, None, 'sp'), may hold values from -3 to 3
- feature_map: bfloat16 [128, 1024], replicated, may hold values from -0.5 to 0.5
- out_gain: float32 [4096], P('sp'), may hold values from 0.25 to 1.75
Outputs:
- attended: bfloat16 [65536, 4096], P(('grp', 'sp'))
All inputs are finite; a program needn't handle non-finite values.
Results may differ from a plain program's by a relative error of at most 0.0052.
Values may be sent and summed in bfloat16 or wider, within the bound.
A program may use at most 128 MiB of HBM per device.

v0:
```python
import jax
import jax.numpy as jnp
from jax import lax
from jax.sharding import PartitionSpec as P

H = 32
DH = 128
CONV = 4
BLOCK = 256


def passed_along(block, axis, distance):
    devices = range(lax.axis_size(axis))
    route = [(i - distance, i) for i in devices if i - distance in devices]
    return lax.ppermute(block, axis, route)


def entering(part, axis, combine, identity):
    place = lax.axis_index(axis)
    gathered = lax.all_gather(part, axis)
    state = jnp.zeros_like(part) + jnp.asarray(identity, part.dtype)

    def one(hop, state):
        return combine(state, lax.dynamic_index_in_dim(gathered, hop, 0, False))

    return lax.fori_loop(0, place, one, state)


def causal_conv(source, earlier, weights):
    tap_count = weights.shape[0]
    length = source.shape[0]
    padded = jnp.concatenate([earlier.astype(jnp.float32), source.astype(jnp.float32)], 0)
    summed = jnp.zeros(source.shape, jnp.float32)
    for tap_index in range(tap_count):
        row_begin = tap_count - 1 - tap_index
        summed = summed + weights[tap_index] * padded[row_begin : row_begin + length]
    return summed.astype(jnp.bfloat16)


def add_states(earlier_total, later_total):
    return earlier_total + later_total


def local(query_input, key_input, value_heads_input, conv_weight, feature_map, out_gain):
    head_count = H // lax.axis_size("sp")
    regrouped = (
        lax.all_to_all(query_input, "sp", split_axis=1, concat_axis=0, tiled=True),
        lax.all_to_all(key_input, "sp", split_axis=1, concat_axis=0, tiled=True),
        lax.all_to_all(value_heads_input, "sp", split_axis=1, concat_axis=0, tiled=True),
    )
    length = regrouped[0].shape[0]
    rim_rows = jnp.stack([member_rows[length - (CONV - 1) :] for member_rows in regrouped])
    earlier_rows = passed_along(rim_rows, "grp", 1)
    block_count = length // BLOCK
    blocked = tuple(
        (
            causal_conv(regrouped[member], earlier_rows[member], conv_weight[member]).reshape(
                block_count, BLOCK, head_count, DH
            )
            for member in range(3)
        )
    )
    causal_mask = lax.iota(jnp.int32, BLOCK)[None, :] <= lax.iota(jnp.int32, BLOCK)[:, None]

    def feature_pass(inputs):
        query_block, key_block, value_tile_rows = inputs
        query_featurized = jnp.maximum(
            jnp.einsum("bhd,dm->bhm", query_block, feature_map, preferred_element_type=jnp.float32),
            0.0,
        ).astype(jnp.bfloat16)
        key_featurized = jnp.maximum(
            jnp.einsum("bhd,dm->bhm", key_block, feature_map, preferred_element_type=jnp.float32),
            0.0,
        ).astype(jnp.bfloat16)
        scores = jnp.einsum(
            "bhm,chm->hbc", query_featurized, key_featurized, preferred_element_type=jnp.float32
        )
        scores = jnp.where(causal_mask[None], scores, 0.0).astype(jnp.bfloat16)
        local_part = jnp.einsum(
            "hbc,chd->bhd", scores, value_tile_rows, preferred_element_type=jnp.float32
        )
        state_increment = jnp.einsum(
            "fzp,fzu->zpu", key_featurized, value_tile_rows, preferred_element_type=jnp.float32
        )
        return (local_part, query_featurized, state_increment)

    local_parts, query_feats, updates = lax.map(feature_pass, blocked)
    group_total = jnp.sum(updates, 0)
    earlier_state = entering(group_total, "grp", add_states, jnp.zeros_like(group_total))
    gain_rows = out_gain.reshape(head_count, DH)

    def finish_block(running_state, inputs):
        query_featurized, state_increment, local_part = inputs
        carried_part = jnp.einsum(
            "srj,rje->sre",
            query_featurized.astype(jnp.float32),
            running_state,
            precision=lax.Precision.HIGHEST,
        )
        numerator = local_part + carried_part
        normed = (
            numerator
            * lax.rsqrt(jnp.mean(numerator * numerator, -1, keepdims=True) + 1e-06)
            * gain_rows
        )
        return (running_state + state_increment, normed.astype(jnp.bfloat16))

    _, finished = lax.scan(finish_block, earlier_state, (query_feats, updates, local_parts))
    attended_output = finished.reshape(length, head_count * DH)
    return lax.all_to_all(attended_output, "sp", split_axis=0, concat_axis=1, tiled=True)


def solution(mesh):
    placed = (
        P(("grp", "sp"), None),
        P(("grp", "sp"), None),
        P(("grp", "sp"), None),
        P(None, None, "sp"),
        P(),
        P("sp"),
    )
    return jax.shard_map(
        local, mesh=mesh, in_specs=placed, out_specs=P(("grp", "sp"), None), check_vma=False
    )
```

profile of v0, /device:TPU:449, one launch (start us, length us, event | category | flops | bytes accessed | tf_op | source)
XLA Modules:
  0.0 380.1 jit_solution(17595038459616549242)
XLA Ops:
  9.0 9.7 %all-to-all-start = ((bf16[128,32,128]{2,0,1:T(8,128)(2,1)}), bf16[128,32,128]{2,0,1:T(8,128)(2,1)S(1)}, u32[]{:S(2)}, u32[]{:S(2)}) async-start(bf16[128,32,128]{2,0,1:T(8,128)(2,1)} %copy_bitcast_fusion.2), calls=%async_computation | async-start | bytes 2097152 | tf_op jit(solution)/shard_map/all_to_all | solution.py:49
  20.0 23.6 %all-to-all-done = bf16[128,32,128]{2,0,1:T(8,128)(2,1)S(1)} async-done(((bf16[128,32,128]{2,0,1:T(8,128)(2,1)}), bf16[128,32,128]{2,0,1:T(8,128)(2,1)S(1)}, u32[]{:S(2)}, u32[]{:S(2)}) %all-to-all-start) | async-done | bytes 1048608 | tf_op jit(solution)/shard_map/all_to_all | solution.py:49
  43.6 8.3 %all-to-all-start.2 = ((bf16[128,32,128]{2,0,1:T(8,128)(2,1)}), bf16[128,32,128]{2,0,1:T(8,128)(2,1)S(1)}, u32[]{:S(2)}, u32[]{:S(2)}) async-start(bf16[128,32,128]{2,0,1:T(8,128)(2,1)} %copy_bitcast_fusion), calls=%async_computation.2 | async-start | bytes 2097152 | tf_op jit(solution)/shard_map/all_to_all | solution.py:48
  51.9 2.5 copy_bitcast_fusion.1
  54.4 22.7 %all-to-all-done.2 = bf16[128,32,128]{2,0,1:T(8,128)(2,1)S(1)} async-done(((bf16[128,32,128]{2,0,1:T(8,128)(2,1)}), bf16[128,32,128]{2,0,1:T(8,128)(2,1)S(1)}, u32[]{:S(2)}, u32[]{:S(2)}) %all-to-all-start.2) | async-done | bytes 1048608 | tf_op jit(solution)/shard_map/all_to_all | solution.py:48
  77.1 8.2 %all-to-all-start.1 = ((bf16[128,32,128]{2,0,1:T(8,128)(2,1)}), bf16[128,32,128]{2,0,1:T(8,128)(2,1)}, u32[]{:S(2)}, u32[]{:S(2)}) async-start(bf16[128,32,128]{2,0,1:T(8,128)(2,1)} %copy_bitcast_fusion.1), calls=%async_computation.1 | async-start | bytes 2097152 | tf_op jit(solution)/shard_map/all_to_all | solution.py:47
  85.4 25.0 %all-to-all-done.1 = bf16[128,32,128]{2,0,1:T(8,128)(2,1)} async-done(((bf16[128,32,128]{2,0,1:T(8,128)(2,1)}), bf16[128,32,128]{2,0,1:T(8,128)(2,1)}, u32[]{:S(2)}, u32[]{:S(2)}) %all-to-all-start.1) | async-done | bytes 1048608 | tf_op jit(solution)/shard_map/all_to_all | solution.py:47
  112.6 1.4 bitcast_convert_fusion.1
  114.2 4.0 %collective-permute-done = bf16[3,3,128]{2,1,0:T(4,128)(2,1)S(1)} collective-permute-done((bf16[3,3,128]{2,1,0:T(4,128)(2,1)S(1)}, bf16[3,3,128]{2,1,0:T(4,128)(2,1)S(1)}, u32[]{:S(2)}, u32[]{:S(2)}) %collective-permute-start) | collective-permute-done | bytes 2336 | tf_op jit(solution)/shard_map/ppermute | solution.py:15
  119.2 3.0 fusion.31
  122.2 85.7 %while.39 = (s32[]{:T(128)}, f32[16,256,1,128]{1,3,2,0:T(8,128)}, bf16[16,256,1,1024]{3,1,2,0:T(8,128)(2,1)}, f32[16,1,1024,128]{3,2,1,0:T(8,128)}, bf16[16,256,...) while((s32[]{:T(128)}, f32[16,256,1,128]{1,3,2,0:T(8,128)}, ...), condition=%wide.region_1.2_spmd.clone, body=%wide.region_0.1_spmd.clone.sunk | while | flops 353566720 | bytes 4591197 | solution.py:87
  122.2 1.9 bitcast_dynamic-update-slice_fusion.2
  127.5 1.9 bitcast_dynamic-update-slice_fusion.2
  132.9 1.9 bitcast_dynamic-update-slice_fusion.2
  138.2 1.9 bitcast_dynamic-update-slice_fusion.2
  143.6 1.9 bitcast_dynamic-update-slice_fusion.2
  149.0 1.9 bitcast_dynamic-update-slice_fusion.2
  154.3 1.9 bitcast_dynamic-update-slice_fusion.2
  159.6 1.9 bitcast_dynamic-update-slice_fusion.2
  165.0 1.9 bitcast_dynamic-update-slice_fusion.2
  170.3 1.9 bitcast_dynamic-update-slice_fusion.2
  175.7 2.0 bitcast_dynamic-update-slice_fusion.2
  181.1 1.9 bitcast_dynamic-update-slice_fusion.2
  186.4 1.9 bitcast_dynamic-update-slice_fusion.2
  191.8 1.9 bitcast_dynamic-update-slice_fusion.2
  197.1 1.9 bitcast_dynamic-update-slice_fusion.2
  202.4 2.0 bitcast_dynamic-update-slice_fusion.2
  207.9 4.6 %reduce_sum.18 = f32[1024,128]{1,0:T(8,128)} reduce(f32[16,1,1024,128]{3,2,1,0:T(8,128)} %get-tuple-element.396, f32[]{:T(128)} %constant.58.clone.1), dimensions={0,1}, to_apply=%region_2.3 | reduce | flops 1966080 | bytes 8912900 | tf_op jit(solution)/shard_map/reduce_sum | solution.py:88
  212.5 54.6 %all-gather.3.cloned.1.call-done = f32[16384,128]{1,0:T(8,128)} async-done(((f32[1024,128]{1,0:T(8,128)}), f32[16384,128]{1,0:T(8,128)}) %all-gather.3.cloned.1.call-update) | async-done | bytes 8388624 | tf_op jit(solution)/shard_map/all_gather | solution.py:20
  267.1 17.8 %while.37 = (s32[]{:T(128)}, f32[1,1024,128]{2,1,0:T(8,128)S(1)}, s32[]{:T(128)}, f32[16,1,1024,128]{3,2,1,0:T(8,128)}, s32[]{:T(128)}, /*index=5*/s32[]{:T(128)}, s32[]{:T(128)}) while((s32[]{:T(128)}, f32[1,1024,128]{2,1,0:T(8,128)S(1)}, s32[]{:T(128)}, f32[16,1,1024,128]{3,2,1,0:T(8,128)}, s32[]{:T(128)}, /*index=5*/s32[]{:T(128)}, ...), condition=%wide.region_4.5_spmd, body=%wide.region_3.4_spmd.sunk | while | flops 131077 | bytes 1572979 | solution.py:26
  284.9 49.6 %while.38 = (s32[]{:T(128)}, f32[1,1024,128]{2,1,0:T(8,128)S(1)}, bf16[16,256,1,128]{3,1,0,2:T(8,128)(2,1)S(1)}, f32[16,1,1024,128]{3,2,1,0:T(8,128)}, f32[16,25...) while((s32[]{:T(128)}, f32[1,1024,128]{2,1,0:T(8,128)S(1)}, ...), condition=%wide.region_7.8_spmd, body=%wide.region_5.7_spmd.sunk | while | flops 402981120 | bytes 3348061 | solution.py:108
  284.9 1.7 multiply_reduce_fusion.2
  288.0 1.7 multiply_reduce_fusion.2
  291.1 1.7 multiply_reduce_fusion.2
  294.2 1.7 multiply_reduce_fusion.2
  297.3 1.7 multiply_reduce_fusion.2
  300.4 1.7 multiply_reduce_fusion.2
  303.5 1.7 multiply_reduce_fusion.2
  306.6 1.7 multiply_reduce_fusion.2
  309.8 1.7 multiply_reduce_fusion.2
  312.9 1.7 multiply_reduce_fusion.2
  316.0 1.7 multiply_reduce_fusion.2
  319.1 1.7 multiply_reduce_fusion.2
  322.2 1.7 multiply_reduce_fusion.2
  325.3 1.7 multiply_reduce_fusion.2
  328.4 1.7 multiply_reduce_fusion.2
  331.5 1.7 multiply_reduce_fusion.2
  334.6 36.7 %all_to_all.76 = bf16[32,128,128]{2,1,0:T(8,128)(2,1)S(1)} all-to-all(bf16[32,128,128]{2,1,0:T(8,128)(2,1)S(1)} %bitcast.184), channel_id=1, replica_groups=mesh['grp'=16,'sp'=32] {'sp'}, dimensions={0} | all-to-all | bytes 2097152 | tf_op jit(solution)/shard_map/all_to_all | solution.py:110
  (174 shorter events, 103.3 us)
Async XLA Ops:
  6.5 1.2 copy-start
  6.5 12.2 %copy-start.2 = (bf16[128,4096]{1,0:T(8,128)(2,1)S(1)}, bf16[128,4096]{1,0:T(8,128)(2,1)}, u32[]{:S(2)}) copy-start(bf16[128,4096]{1,0:T(8,128)(2,1)} %param.13) | copy-start | bytes 3145732
  9.0 34.5 %all-to-all-start = ((bf16[128,32,128]{2,0,1:T(8,128)(2,1)}), bf16[128,32,128]{2,0,1:T(8,128)(2,1)S(1)}, u32[]{:S(2)}, u32[]{:S(2)}) async-start(bf16[128,32,128]{2,0,1:T(8,128)(2,1)} %copy_bitcast_fusion.2), calls=%async_computation | async-start | bytes 2097152 | tf_op jit(solution)/shard_map/all_to_all | solution.py:49
  43.6 33.5 %all-to-all-start.2 = ((bf16[128,32,128]{2,0,1:T(8,128)(2,1)}), bf16[128,32,128]{2,0,1:T(8,128)(2,1)S(1)}, u32[]{:S(2)}, u32[]{:S(2)}) async-start(bf16[128,32,128]{2,0,1:T(8,128)(2,1)} %copy_bitcast_fusion), calls=%async_computation.2 | async-start | bytes 2097152 | tf_op jit(solution)/shard_map/all_to_all | solution.py:48
  51.9 33.4 %copy-start.4 = (f32[3,4,128]{2,1,0:T(4,128)S(1)}, f32[3,4,128]{2,1,0:T(4,128)}, u32[]{:S(2)}) copy-start(f32[3,4,128]{2,1,0:T(4,128)} %param.15) | copy-start | bytes 18436
  77.1 33.3 %all-to-all-start.1 = ((bf16[128,32,128]{2,0,1:T(8,128)(2,1)}), bf16[128,32,128]{2,0,1:T(8,128)(2,1)}, u32[]{:S(2)}, u32[]{:S(2)}) async-start(bf16[128,32,128]{2,0,1:T(8,128)(2,1)} %copy_bitcast_fusion.1), calls=%async_computation.1 | async-start | bytes 2097152 | tf_op jit(solution)/shard_map/all_to_all | solution.py:47
  85.3 181.8 %all-gather.3.cloned.1.call-start = ((), (), s32[]{:S(2)}) async-start(), calls=%async_computation.4 | async-start | bytes 8912896 | tf_op jit(solution)/shard_map/all_gather | solution.py:20
  111.1 7.1 %collective-permute-start = (bf16[3,3,128]{2,1,0:T(4,128)(2,1)S(1)}, bf16[3,3,128]{2,1,0:T(4,128)(2,1)S(1)}, u32[]{:S(2)}, u32[]{:S(2)}) collective-permute-start(bf16[3,3,128]{2,1,0:T(4,128)(2,1)S(1)} %pad_maximum_fusion.3), channel_id=1, source_target_pairs={{0,32},{32,64},{64,96},{96,128},{128,160},{160,192},{192,224},{224... | collective-permute-start | bytes 6920 | tf_op jit(solution)/shard_map/ppermute | solution.py:15
  119.2 3.0 copy-start.1
  267.1 17.8 %copy-start.3 = (f32[128]{0:T(128)S(1)}, f32[128]{0:T(128)}, u32[]{:S(2)}) copy-start(f32[128]{0:T(128)} %param.17) | copy-start | bytes 1540
Sparse Core Ops, SparseCore 0:
  212.6 54.4 all-gather.2
where the time goes:
time: 385 us; the launch traced here: 380 us
  waiting for transfers between devices  130 us (34%)
  matrix products  112 us (29%)
  other arithmetic  47.7 us (12%)
  blocking collectives  36.7 us (10%)
  starting transfers between devices  27.5 us (7%)
  between operations  13.6 us (4%)
  local copies, waits for them, and re-layouts  11.1 us (3%)
    all_gather x1, waiting for transfers between devices, entering(): gathered = lax.all_gather(part, axis)  54.6 us
    all_to_all x1, blocking collectives, local(): lax.all_to_all(attended_output, 'sp', split_axis=0, concat_axis=1, tiled=...  36.7 us
    dot_general x16, matrix products, feature_pass(): jnp.einsum('bhd,dm->bhm', query_block, feature_map, preferred_element_typ...  30.9 us
    dot_general x16, matrix products, finish_block(): jnp.einsum('srj,rje->sre', query_featurized.astype(jnp.float32), running_...  26.8 us
    all_to_all x1, waiting for transfers between devices, local(): lax.all_to_all(query_input, 'sp', split_axis=1, concat_axis=0, tiled=True)  25 us
    all_to_all x1, waiting for transfers between devices, local(): lax.all_to_all(value_heads_input, 'sp', split_axis=1, concat_axis=0, tile...  23.6 us
    all_to_all x1, waiting for transfers between devices, local(): lax.all_to_all(key_input, 'sp', split_axis=1, concat_axis=0, tiled=True)  22.7 us
    dot_general x16, matrix products, feature_pass(): jnp.einsum('fzp,fzu->zpu', key_featurized, value_tile_rows, preferred_ele...  18.6 us
  transfers between devices with their start and end apart: 5, of which 5 were waited for; matrix products, arithmetic and copies ran while one was open for 1% of the time, Pallas kernels for 0%

commit v1 on v0

v1 whole, which is shorter than its diff:
```python
import functools

import jax
import jax.numpy as jnp
from jax import lax
from jax.experimental import pallas as pl
from jax.experimental.pallas import tpu as pltpu
from jax.sharding import PartitionSpec as P

DH = 128
CONV = 4
BLOCK = 256
CHUNK = 128
HALO = 16
MESH = pl.DeviceIdType.MESH
F32 = jnp.float32
BF16 = jnp.bfloat16
CONTRACT_LAST = (((1,), (1,)), ((), ()))
CONTRACT_FIRST = (((0,), (0,)), ((), ()))
Q, K, V = 0, 1, 2


def kernel(
    nsp,
    ngrp,
    q_hbm,
    k_hbm,
    v_hbm,
    cw_ref,
    fm_ref,
    gain_ref,
    out_hbm,
    qbuf,
    kbuf,
    vbuf,
    qf,
    kf,
    vc,
    upd,
    loc,
    obuf,
    total,
    tsend,
    tin,
    psend,
    prx,
    esend,
    ein,
    est,
    in_send,
    in_recv,
    halo_send,
    halo_recv,
    core_send,
    core_recv,
    z_send,
    z_recv,
    out_send,
    out_recv,
):
    nb = nsp // 2
    nz = ngrp // 2
    m = fm_ref.shape[1]
    me = lax.axis_index("sp")
    g = lax.axis_index("grp")
    z, core = g // 2, lax.rem(g, 2)
    b0 = me // 2
    partner = g + 1 - 2 * core
    following = lax.rem(g + 1, ngrp)
    hbm = (q_hbm, k_hbm, v_hbm)
    bufs = (qbuf, kbuf, vbuf)

    barrier = pltpu.get_barrier_semaphore()

    @pl.loop(1, nsp)
    def _(i):
        pl.semaphore_signal(
            barrier, inc=1, device_id={"sp": lax.rem(me + i, nsp)}, device_id_type=MESH
        )

    @pl.loop(1, ngrp)
    def _(i):
        pl.semaphore_signal(
            barrier, inc=1, device_id={"grp": lax.rem(g + i, ngrp)}, device_id_type=MESH
        )

    pl.semaphore_wait(barrier, nsp + ngrp - 2)

    def rows_of(chunk):
        return pl.ds(pl.multiple_of(HALO + chunk * CHUNK, 16), CHUNK)

    def columns_of(head):
        return pl.ds(pl.multiple_of(head * DH, DH), DH)

    def input_copy(t, d):
        return pltpu.make_async_remote_copy(
            src_ref=hbm[t].at[:, columns_of(d)],
            dst_ref=bufs[t].at[rows_of(me)],
            send_sem=in_send.at[t, d],
            recv_sem=in_recv.at[t, me],
            device_id={"sp": d},
            device_id_type=MESH,
        )

    def own_copy(t):
        return pltpu.make_async_copy(
            hbm[t].at[:, columns_of(me)], bufs[t].at[rows_of(me)], in_recv.at[t, me]
        )

    def send_inputs(tensors):
        for t in tensors:
            own_copy(t).start()
        for t in tensors:
            input_copy(t, me + 1 - 2 * lax.rem(me, 2)).start()

        @pl.loop(1, nb)
        def _(i):
            pair = lax.rem(b0 + nb - i, nb)
            for e in range(2):
                for t in tensors:
                    input_copy(t, 2 * pair + e).start()

    def halo_copy(t):
        return pltpu.make_async_remote_copy(
            src_ref=bufs[t].at[pl.ds(nsp * CHUNK, HALO)],
            dst_ref=bufs[t].at[pl.ds(0, HALO)],
            send_sem=halo_send.at[t],
            recv_sem=halo_recv.at[t],
            device_id={"grp": following},
            device_id_type=MESH,
        )

    def arrive(b, tensors):
        for t in tensors:
            for e in range(2):
                rows = bufs[t].at[rows_of(2 * b + e)]
                pltpu.make_async_copy(rows, rows, in_recv.at[t, 2 * b + e]).wait()

        @pl.when(b == nb - 1)
        def _():
            for t in tensors:
                halo_copy(t).start()

    def halo_ready(b, tensors):
        @pl.when(b == 0)
        def _():
            for t in tensors:
                halo_copy(t).wait_recv()

            @pl.when(g == 0)
            def _():
                for t in tensors:
                    bufs[t][pl.ds(0, HALO), :] = jnp.zeros((HALO, DH), BF16)

    def conv(t, b):
        rows = bufs[t][pl.ds(pl.multiple_of(b * BLOCK, BLOCK), BLOCK + HALO), :].astype(F32)
        summed = cw_ref[t, 0:1, :] * rows[HALO:]
        for j in range(1, CONV):
            summed = summed + cw_ref[t, j : j + 1, :] * pltpu.roll(rows, j, 0)[HALO:]
        return summed.astype(BF16)

    def featurize(rows, dst, b):
        for j in range(0, m, 256):
            f = jnp.dot(rows, fm_ref[:, j : j + 256], preferred_element_type=F32)
            dst[b, :, j : j + 256] = jnp.maximum(f, 0.0).astype(BF16)

    def block_rows(b):
        return pl.ds(pl.multiple_of(b * BLOCK, BLOCK), BLOCK)

    send_inputs((K, V))
    send_inputs((Q,))

    total[...] = jnp.zeros_like(total)

    def key_block(b):
        halo_ready(b, (K, V))
        value = conv(V, b)
        vc[block_rows(b), :] = value
        featurize(conv(K, b), kf, b)
        increment = lax.dot_general(value, kf[b], CONTRACT_FIRST, preferred_element_type=F32)
        upd[b] = increment
        total[...] += increment

    arrive(b0, (K, V))

    @pl.loop(1, nb)
    def _(i):
        b = lax.rem(b0 + i, nb)
        arrive(b, (K, V))
        key_block(b)

    key_block(b0)

    half = DH // 2
    mine = pl.ds(pl.multiple_of(core * half, half), half)
    theirs = pl.ds(pl.multiple_of((1 - core) * half, half), half)

    def core_copy(k, src, dst):
        return pltpu.make_async_remote_copy(
            src_ref=src,
            dst_ref=dst,
            send_sem=core_send.at[k],
            recv_sem=core_recv.at[k],
            device_id={"grp": partner},
            device_id_type=MESH,
        )

    tsend[...] = total[theirs, :].astype(BF16)
    first = core_copy(0, tsend, tin)
    first.start()

    def exclusive(b, running):
        increment = upd[b]
        upd[b] = est[...]
        est[...] += increment
        return running

    est[...] = jnp.zeros_like(est)
    lax.fori_loop(0, nb, exclusive, 0)

    first.wait_recv()
    psend[...] = (total[mine, :] + tin[...].astype(F32)).astype(BF16)

    def z_copy(to):
        return pltpu.make_async_remote_copy(
            src_ref=psend,
            dst_ref=prx.at[z],
            send_sem=z_send.at[to],
            recv_sem=z_recv.at[z],
            device_id={"grp": 2 * to + core},
            device_id_type=MESH,
        )

    @pl.loop(1, nz)
    def _(i):
        @pl.when(z + i < nz)
        def _():
            z_copy(z + i).start()

    row_at = lax.broadcasted_iota(jnp.int32, (BLOCK, BLOCK), 0)
    column_at = lax.broadcasted_iota(jnp.int32, (BLOCK, BLOCK), 1)

    def query_block(b):
        halo_ready(b, (Q,))
        featurize(conv(Q, b), qf, b)
        scores = lax.dot_general(qf[b], kf[b], CONTRACT_LAST, preferred_element_type=F32)
        scores = jnp.where(column_at <= row_at, scores, 0.0).astype(BF16)
        loc[block_rows(b), :] = jnp.dot(
            scores, vc[block_rows(b), :], preferred_element_type=F32
        )

    arrive(b0, (Q,))

    @pl.loop(1, nb)
    def _(i):
        b = lax.rem(b0 + i, nb)
        arrive(b, (Q,))
        query_block(b)

    query_block(b0)

    est[mine, :] = jnp.zeros((half, m), F32)

    @pl.loop(0, nz)
    def _(i):
        @pl.when(i < z)
        def _():
            slot = prx.at[i]
            pltpu.make_async_copy(slot, slot, z_recv.at[i]).wait()
            est[mine, :] += prx[i].astype(F32)

    @pl.when(core == 0)
    def _():
        esend[...] = (est[mine, :] + total[mine, :]).astype(BF16)

    @pl.when(core == 1)
    def _():
        esend[...] = est[mine, :].astype(BF16)
        est[mine, :] += tin[...].astype(F32)

    second = core_copy(1, esend, ein)
    second.start()
    second.wait_recv()
    est[theirs, :] = ein[...].astype(F32)

    def out_copy(d):
        return pltpu.make_async_remote_copy(
            src_ref=obuf.at[pl.ds(pl.multiple_of(d * CHUNK, CHUNK), CHUNK)],
            dst_ref=out_hbm.at[:, columns_of(me)],
            send_sem=out_send.at[d],
            recv_sem=out_recv.at[me],
            device_id={"sp": d},
            device_id_type=MESH,
        )

    def finish(b):
        state = (est[...] + upd[b]).astype(BF16)
        numerator = loc[block_rows(b), :] + lax.dot_general(
            qf[b], state, CONTRACT_LAST, preferred_element_type=F32
        )
        scale = lax.rsqrt(jnp.mean(numerator * numerator, -1, keepdims=True) + 1e-06)
        obuf[block_rows(b), :] = (numerator * scale * gain_ref[...]).astype(BF16)

    finish(b0)
    pltpu.make_async_copy(
        obuf.at[pl.ds(pl.multiple_of(me * CHUNK, CHUNK), CHUNK)],
        out_hbm.at[:, columns_of(me)],
        out_recv.at[me],
    ).start()
    out_copy(me + 1 - 2 * lax.rem(me, 2)).start()

    @pl.loop(1, nb)
    def _(i):
        b = lax.rem(b0 + i, nb)
        finish(b)
        for e in range(2):
            out_copy(2 * b + e).start()

    @pl.loop(0, nsp)
    def _(s):
        block = out_hbm.at[:, columns_of(s)]
        pltpu.make_async_copy(block, block, out_recv.at[s]).wait()

    @pl.loop(1, nsp)
    def _(i):
        d = lax.rem(me + i, nsp)
        for t in (K, V, Q):
            input_copy(t, d).wait_send()
        out_copy(d).wait_send()

    for t in (K, V, Q):
        halo_copy(t).wait_send()
    first.wait_send()
    second.wait_send()

    @pl.loop(1, nz)
    def _(i):
        @pl.when(z + i < nz)
        def _():
            z_copy(z + i).wait_send()


def solution(mesh):
    nsp, ngrp = mesh.shape["sp"], mesh.shape["grp"]

    def local(query_input, key_input, value_heads_input, conv_weight, feature_map, out_gain):
        length = nsp * CHUNK
        nb = nsp // 2
        m = feature_map.shape[1]
        any_spec = pl.BlockSpec(memory_space=pl.ANY)
        vmem_spec = pl.BlockSpec(memory_space=pltpu.VMEM)
        dma = pltpu.SemaphoreType.DMA
        return pl.pallas_call(
            functools.partial(kernel, nsp, ngrp),
            out_shape=jax.ShapeDtypeStruct(query_input.shape, BF16),
            in_specs=[any_spec] * 3 + [vmem_spec] * 3,
            out_specs=any_spec,
            scratch_shapes=[
                pltpu.VMEM((HALO + length, DH), BF16),
                pltpu.VMEM((HALO + length, DH), BF16),
                pltpu.VMEM((HALO + length, DH), BF16),
                pltpu.VMEM((nb, BLOCK, m), BF16),
                pltpu.VMEM((nb, BLOCK, m), BF16),
                pltpu.VMEM((length, DH), BF16),
                pltpu.VMEM((nb, DH, m), F32),
                pltpu.VMEM((length, DH), F32),
                pltpu.VMEM((length, DH), BF16),
                pltpu.VMEM((DH, m), F32),
                pltpu.VMEM((DH // 2, m), BF16),
                pltpu.VMEM((DH // 2, m), BF16),
                pltpu.VMEM((DH // 2, m), BF16),
                pltpu.VMEM((ngrp // 2, DH // 2, m), BF16),
                pltpu.VMEM((DH // 2, m), BF16),
                pltpu.VMEM((DH // 2, m), BF16),
                pltpu.VMEM((DH, m), F32),
                dma((3, nsp)),
                dma((3, nsp)),
                dma((3,)),
                dma((3,)),
                dma((2,)),
                dma((2,)),
                dma((ngrp // 2,)),
                dma((ngrp // 2,)),
                dma((nsp,)),
                dma((nsp,)),
            ],
            compiler_params=pltpu.CompilerParams(
                collective_id=0, has_side_effects=True, vmem_limit_bytes=56 << 20
            ),
        )(
            query_input,
            key_input,
            value_heads_input,
            conv_weight,
            feature_map,
            out_gain.reshape(1, DH),
        )

    placed = (
        P(("grp", "sp"), None),
        P(("grp", "sp"), None),
        P(("grp", "sp"), None),
        P(None, None, "sp"),
        P(),
        P("sp"),
    )
    return jax.shard_map(
        local, mesh=mesh, in_specs=placed, out_specs=P(("grp", "sp"), None), check_vma=False
    )
```

time: 385 us -> 128 us (0.33)
  the two profiles are of different devices: /device:TPU:449 before, /device:TPU:215 now
where the time goes in v1:
time: 128 us
  Pallas kernels  125 us (98%)
  local copies, waits for them, and re-layouts  2.29 us (2%)
    pallas_call x1, Pallas kernels, local(): pl.pallas_call(functools.partial(kernel, nsp, ngrp), out_shape=jax.ShapeD...  125 us

profile of v1, /device:TPU:215, one launch (start us, length us, event | category | flops | bytes accessed | tf_op | source)
XLA Modules:
  0.0 127.6 jit_solution(5367778450924138635)
XLA Ops:
  0.0 125.3 %shard_map.64 = bf16[128,4096]{1,0:T(8,128)(2,1)} custom-call(bf16[128,4096]{1,0:T(8,128)(2,1)} %q_hbm.1, bf16[128,4096]{1,0:T(8,128)(2,1)} %k_hbm.1, bf16[128,4096]{1,0:T(8,128)(2,1)} %v_hbm.1, f32[3,4,128]{2,1,0:T(4,128)} %cw_ref.1, bf16[128,1024]{1,0:T(8,128)(2,1)} %fm_ref.1, f32[1,128]{1,0:T(1,128)} %bitcast.1), custom_call_target="tpu_custom_call" | custom-call | tf_op jit(solution)/shard_map/pallas_call | solution.py:353
  125.4 2.3 %copy.8 = bf16[128,4096]{1,0:T(8,128)(2,1)} copy(bf16[128,4096]{1,0:T(8,128)(2,1)} %shard_map.64) | data formatting | bytes 2097152

commit v2 on v1

v2 whole, which is shorter than its diff:
```python
import functools

import jax
import jax.numpy as jnp
from jax import lax
from jax.experimental import pallas as pl
from jax.experimental.pallas import tpu as pltpu
from jax.sharding import PartitionSpec as P

DH = 128
CONV = 4
BLOCK = 256
CHUNK = 128
HALO = 16
SLICES = 8
MESH = pl.DeviceIdType.MESH
F32 = jnp.float32
BF16 = jnp.bfloat16
CONTRACT_LAST = (((1,), (1,)), ((), ()))
CONTRACT_FIRST = (((0,), (0,)), ((), ()))
Q, K, V = 0, 1, 2


def kernel(
    nsp,
    ngrp,
    q_hbm,
    k_hbm,
    v_hbm,
    cw_hbm,
    fm_hbm,
    gain_hbm,
    out_hbm,
    qbuf,
    kbuf,
    vbuf,
    qf,
    kf,
    vc,
    upd,
    loc,
    obuf,
    total,
    tsend,
    tin,
    chain_out,
    chain_in,
    pair_out,
    pair_in,
    est,
    cw_ref,
    fm_ref,
    gain_ref,
    in_send,
    in_recv,
    halo_send,
    halo_recv,
    chain_send,
    chain_recv,
    pair_send,
    pair_recv,
    above,
    out_send,
    out_recv,
    weight_sem,
):
    nb = nsp // 2
    m = fm_hbm.shape[1]
    me = lax.axis_index("sp")
    g = lax.axis_index("grp")
    b0 = me // 2
    nz = ngrp // 2
    z, core = g // 2, lax.rem(g, 2)
    partner = g + 1 - 2 * core
    hbm = (q_hbm, k_hbm, v_hbm)
    bufs = (qbuf, kbuf, vbuf)

    barrier = pltpu.get_barrier_semaphore()

    def greet(semaphore, **device):
        pl.semaphore_signal(semaphore, inc=1, device_id=device, device_id_type=MESH)

    @pl.loop(1, nsp)
    def _(i):
        greet(barrier, sp=lax.rem(me + i, nsp))

    greet(barrier, grp=partner)

    @pl.when(g + 2 < ngrp)
    def _():
        greet(barrier, grp=g + 2)

    @pl.when(jnp.logical_and(core == 1, g + 1 < ngrp))
    def _():
        greet(barrier, grp=g + 1)

    weights = [
        pltpu.make_async_copy(src, dst, weight_sem.at[i])
        for i, (src, dst) in enumerate(
            ((cw_hbm, cw_ref), (fm_hbm, fm_ref), (gain_hbm, gain_ref))
        )
    ]
    for copy in weights:
        copy.start()
    pl.semaphore_wait(barrier, nsp + jnp.where(z > 0, 2 - core, 0))

    @pl.when(z > 0)
    def _():
        greet(above, grp=g - 2)

    @pl.when(jnp.logical_and(core == 0, z > 0))
    def _():
        greet(above, grp=g - 1)

    def rows_of(chunk):
        return pl.ds(pl.multiple_of(HALO + chunk * CHUNK, 16), CHUNK)

    def columns_of(head):
        return pl.ds(pl.multiple_of(head * DH, DH), DH)

    def input_copy(t, d):
        return pltpu.make_async_remote_copy(
            src_ref=hbm[t].at[:, columns_of(d)],
            dst_ref=bufs[t].at[rows_of(me)],
            send_sem=in_send.at[t, d],
            recv_sem=in_recv.at[t, me],
            device_id={"sp": d},
            device_id_type=MESH,
        )

    def own_copy(t):
        return pltpu.make_async_copy(
            hbm[t].at[:, columns_of(me)], bufs[t].at[rows_of(me)], in_recv.at[t, me]
        )

    def send_inputs(tensors):
        for t in tensors:
            own_copy(t).start()
        for t in tensors:
            input_copy(t, me + 1 - 2 * lax.rem(me, 2)).start()

        @pl.loop(1, nb)
        def _(i):
            step = jnp.where(b0 == nb - 1, lax.rem(i + nb - 3, nb - 1) + 1, i)
            pair = lax.rem(b0 + nb - step, nb)
            for e in range(2):
                for t in tensors:
                    input_copy(t, 2 * pair + e).start()

    def halo_copy(t):
        return pltpu.make_async_remote_copy(
            src_ref=bufs[t].at[pl.ds(nsp * CHUNK, HALO)],
            dst_ref=bufs[t].at[pl.ds(0, HALO)],
            send_sem=halo_send.at[t],
            recv_sem=halo_recv.at[t],
            device_id={"grp": g + 1},
            device_id_type=MESH,
        )

    def arrive(b, tensors):
        for t in tensors:
            for e in range(2):
                rows = bufs[t].at[rows_of(2 * b + e)]
                pltpu.make_async_copy(rows, rows, in_recv.at[t, 2 * b + e]).wait()

        @pl.when(jnp.logical_and(b == nb - 1, g + 1 < ngrp))
        def _():
            for t in tensors:
                halo_copy(t).start()

    def halo_ready(b, tensors):
        @pl.when(jnp.logical_and(b == 0, g > 0))
        def _():
            for t in tensors:
                halo = bufs[t].at[pl.ds(0, HALO)]
                pltpu.make_async_copy(halo, halo, halo_recv.at[t]).wait()

    def conv(t, b):
        rows = bufs[t][pl.ds(pl.multiple_of(b * BLOCK, BLOCK), BLOCK + HALO), :].astype(F32)
        summed = cw_ref[t, 0:1, :] * rows[HALO:]
        for j in range(1, CONV):
            summed = summed + cw_ref[t, j : j + 1, :] * pltpu.roll(rows, j, 0)[HALO:]
        return summed.astype(BF16)

    def featurize(rows, dst, b):
        for j in range(0, m, 256):
            f = jnp.dot(rows, fm_ref[:, j : j + 256], preferred_element_type=F32)
            dst[b, :, j : j + 256] = jnp.maximum(f, 0.0).astype(BF16)

    def block_rows(b):
        return pl.ds(pl.multiple_of(b * BLOCK, BLOCK), BLOCK)

    send_inputs((K, V))
    send_inputs((Q,))

    @pl.when(g == 0)
    def _():
        for t in (K, V, Q):
            bufs[t][pl.ds(0, HALO), :] = jnp.zeros((HALO, DH), BF16)

    @pl.when(z + 1 < nz)
    def _():
        pl.semaphore_wait(above, 1 + core)

    total[...] = jnp.zeros_like(total)
    for copy in weights:
        copy.wait()

    def key_block(b):
        halo_ready(b, (K, V))
        value = conv(V, b)
        vc[block_rows(b), :] = value
        featurize(conv(K, b), kf, b)
        increment = lax.dot_general(value, kf[b], CONTRACT_FIRST, preferred_element_type=F32)
        upd[b] = increment
        total[...] += increment

    def arrive_first(tensors):
        arrive(b0, tensors)

        @pl.when(b0 == 0)
        def _():
            arrive(nb - 1, tensors)

    def arrive_next(i, b, tensors):
        @pl.when(jnp.logical_or(b0 > 0, i < nb - 1))
        def _():
            arrive(b, tensors)

    arrive_first((K, V))

    @pl.loop(1, nb)
    def _(i):
        b = lax.rem(b0 + i, nb)
        arrive_next(i, b, (K, V))
        key_block(b)

    key_block(b0)

    slices, slice_rows, slice_columns = chain_in.shape
    splits = m // slice_columns
    half = DH // 2

    def place(of, s):
        row = pl.multiple_of(of * half + s // splits * slice_rows, slice_rows)
        column = s % splits * slice_columns
        return pl.ds(row, slice_rows), slice(column, column + slice_columns)

    def pair_copy(k, src, dst):
        return pltpu.make_async_remote_copy(
            src_ref=src,
            dst_ref=dst,
            send_sem=pair_send.at[k],
            recv_sem=pair_recv.at[k],
            device_id={"grp": partner},
            device_id_type=MESH,
        )

    def chain_copy(s):
        return pltpu.make_async_remote_copy(
            src_ref=chain_out.at[s],
            dst_ref=chain_in.at[s],
            send_sem=chain_send.at[s],
            recv_sem=chain_recv.at[s],
            device_id={"grp": g + 2},
            device_id_type=MESH,
        )

    for s in range(slices):
        tsend[s] = total[place(1 - core, s)].astype(BF16)
    first = pair_copy(slices, tsend, tin)
    first.start()

    @pl.when(z == 0)
    def _():
        chain_in[...] = jnp.zeros_like(chain_in)

    def exclusive(b, running):
        increment = upd[b]
        upd[b] = est[...]
        est[...] += increment
        return running

    def exclusive_pass():
        est[...] = jnp.zeros_like(est)
        lax.fori_loop(0, nb, exclusive, 0)

    @pl.when(z >= 3)
    def _():
        exclusive_pass()

    first.wait_recv()
    lower = (1 - core).astype(F32)

    for s in range(slices):

        @pl.when(z > 0)
        def _():
            slot = chain_in.at[s]
            pltpu.make_async_copy(slot, slot, chain_recv.at[s]).wait()

        earlier = chain_in[s].astype(F32)
        own, other = total[place(core, s)], tin[s].astype(F32)

        @pl.when(z + 1 < nz)
        def _():
            chain_out[s] = (earlier + (own + other)).astype(BF16)
            chain_copy(s).start()

        pair_out[s] = (earlier + lower * own).astype(BF16)
        pair_copy(s, pair_out.at[s], pair_in.at[s]).start()

    @pl.when(z < 3)
    def _():
        exclusive_pass()

    for s in range(slices):
        other = tin[s].astype(F32)
        est[place(core, s)] = chain_in[s].astype(F32) + (1.0 - lower) * other

    row_at = lax.broadcasted_iota(jnp.int32, (BLOCK, BLOCK), 0)
    column_at = lax.broadcasted_iota(jnp.int32, (BLOCK, BLOCK), 1)

    def query_block(b):
        halo_ready(b, (Q,))
        featurize(conv(Q, b), qf, b)
        scores = lax.dot_general(qf[b], kf[b], CONTRACT_LAST, preferred_element_type=F32)
        scores = jnp.where(column_at <= row_at, scores, 0.0).astype(BF16)
        loc[block_rows(b), :] = jnp.dot(
            scores, vc[block_rows(b), :], preferred_element_type=F32
        )

    def query_step(i):
        b = lax.rem(b0 + i, nb)
        arrive_next(i, b, (Q,))
        query_block(b)

    arrive_first((Q,))
    for s in range(slices):
        pair_copy(s, pair_out.at[s], pair_in.at[s]).wait_recv()
        est[place(1 - core, s)] = pair_in[s].astype(F32)

    def out_copy(d):
        return pltpu.make_async_remote_copy(
            src_ref=obuf.at[pl.ds(pl.multiple_of(d * CHUNK, CHUNK), CHUNK)],
            dst_ref=out_hbm.at[:, columns_of(me)],
            send_sem=out_send.at[d],
            recv_sem=out_recv.at[me],
            device_id={"sp": d},
            device_id_type=MESH,
        )

    def finish(b):
        state = (est[...] + upd[b]).astype(BF16)
        numerator = loc[block_rows(b), :] + lax.dot_general(
            qf[b], state, CONTRACT_LAST, preferred_element_type=F32
        )
        scale = lax.rsqrt(jnp.mean(numerator * numerator, -1, keepdims=True) + 1e-06)
        obuf[block_rows(b), :] = (numerator * scale * gain_ref[...]).astype(BF16)

    @pl.loop(1, nb)
    def _(i):
        b = lax.rem(b0 + i, nb)
        arrive_next(i, b, (Q,))
        query_block(b)
        finish(b)
        for e in range(2):
            out_copy(2 * b + e).start()

    query_block(b0)
    finish(b0)
    out_copy(me + 1 - 2 * lax.rem(me, 2)).start()
    pltpu.make_async_copy(
        obuf.at[pl.ds(pl.multiple_of(me * CHUNK, CHUNK), CHUNK)],
        out_hbm.at[:, columns_of(me)],
        out_recv.at[me],
    ).start()

    @pl.loop(0, nsp)
    def _(s):
        block = out_hbm.at[:, columns_of(s)]
        pltpu.make_async_copy(block, block, out_recv.at[s]).wait()

    @pl.loop(1, nsp)
    def _(i):
        d = lax.rem(me + i, nsp)
        for t in (K, V, Q):
            input_copy(t, d).wait_send()
        out_copy(d).wait_send()

    @pl.when(g + 1 < ngrp)
    def _():
        for t in (K, V, Q):
            halo_copy(t).wait_send()

    first.wait_send()
    for s in range(slices):
        pair_copy(s, pair_out.at[s], pair_in.at[s]).wait_send()

        @pl.when(z + 1 < nz)
        def _():
            chain_copy(s).wait_send()


def solution(mesh):
    nsp, ngrp = mesh.shape["sp"], mesh.shape["grp"]

    def local(query_input, key_input, value_heads_input, conv_weight, feature_map, out_gain):
        length = nsp * CHUNK
        nb = nsp // 2
        m = feature_map.shape[1]
        pieces = (SLICES, HALO, DH // 2 * m // (HALO * SLICES))
        any_spec = pl.BlockSpec(memory_space=pl.ANY)
        dma = pltpu.SemaphoreType.DMA
        return pl.pallas_call(
            functools.partial(kernel, nsp, ngrp),
            out_shape=jax.ShapeDtypeStruct(query_input.shape, BF16),
            in_specs=[any_spec] * 6,
            out_specs=any_spec,
            scratch_shapes=[
                pltpu.VMEM((HALO + length, DH), BF16),
                pltpu.VMEM((HALO + length, DH), BF16),
                pltpu.VMEM((HALO + length, DH), BF16),
                pltpu.VMEM((nb, BLOCK, m), BF16),
                pltpu.VMEM((nb, BLOCK, m), BF16),
                pltpu.VMEM((length, DH), BF16),
                pltpu.VMEM((nb, DH, m), F32),
                pltpu.VMEM((length, DH), F32),
                pltpu.VMEM((length, DH), BF16),
                pltpu.VMEM((DH, m), F32),
                pltpu.VMEM(pieces, BF16),
                pltpu.VMEM(pieces, BF16),
                pltpu.VMEM(pieces, BF16),
                pltpu.VMEM(pieces, BF16),
                pltpu.VMEM(pieces, BF16),
                pltpu.VMEM(pieces, BF16),
                pltpu.VMEM((DH, m), F32),
                pltpu.VMEM(conv_weight.shape, F32),
                pltpu.VMEM(feature_map.shape, BF16),
                pltpu.VMEM((1, DH), F32),
                dma((3, nsp)),
                dma((3, nsp)),
                dma((3,)),
                dma((3,)),
                dma((SLICES,)),
                dma((SLICES,)),
                dma((SLICES + 1,)),
                dma((SLICES + 1,)),
                pltpu.SemaphoreType.REGULAR,
                dma((nsp,)),
                dma((nsp,)),
                dma((3,)),
            ],
            compiler_params=pltpu.CompilerParams(
                collective_id=0, has_side_effects=True, vmem_limit_bytes=56 << 20
            ),
        )(
            query_input,
            key_input,
            value_heads_input,
            conv_weight,
            feature_map,
            out_gain.reshape(1, DH),
        )

    placed = (
        P(("grp", "sp"), None),
        P(("grp", "sp"), None),
        P(("grp", "sp"), None),
        P(None, None, "sp"),
        P(),
        P("sp"),
    )
    return jax.shard_map(
        local, mesh=mesh, in_specs=placed, out_specs=P(("grp", "sp"), None), check_vma=False
    )
```

time: 128 us -> 111 us (0.87)
  the two profiles are of different devices: /device:TPU:215 before, /device:TPU:449 now
where the time goes in v2:
time: 111 us
  Pallas kernels  108 us (97%)
  local copies, waits for them, and re-layouts  2.29 us (2%)
    pallas_call x1, Pallas kernels, local(): pl.pallas_call(functools.partial(kernel, nsp, ngrp), out_shape=jax.ShapeD...  108 us
    unnamed x1, local copies, waits for them, and re-layouts  2.29 us

profile of v2, /device:TPU:449, one launch (start us, length us, event | category | flops | bytes accessed | tf_op | source)
XLA Modules:
  0.0 110.7 jit_solution(12200876172457651056)
XLA Ops:
  0.0 108.4 %shard_map.64 = bf16[128,4096]{1,0:T(8,128)(2,1)} custom-call(bf16[128,4096]{1,0:T(8,128)(2,1)} %q_hbm.1, bf16[128,4096]{1,0:T(8,128)(2,1)} %k_hbm.1, bf16[128,4096]{1,0:T(8,128)(2,1)} %v_hbm.1, f32[3,4,128]{2,1,0:T(4,128)} %cw_hbm.1, bf16[128,1024]{1,0:T(8,128)(2,1)} %fm_hbm.1, f32[1,128]{1,0:T(1,128)} %bitcast.1), custom_call_target="tpu_custom_call" | custom-call | tf_op jit(solution)/shard_map/pallas_call | solution.py:415
  108.4 2.3 %copy.8 = bf16[128,4096]{1,0:T(8,128)(2,1)} copy(bf16[128,4096]{1,0:T(8,128)(2,1)} %shard_map.64) | data formatting | bytes 2097152

commit v3 on v2

--- a/solution.py
+++ b/solution.py
@@ -237,6 +237,23 @@
 
     key_block(b0)
 
+    row_at = lax.broadcasted_iota(jnp.int32, (BLOCK, BLOCK), 0)
+    column_at = lax.broadcasted_iota(jnp.int32, (BLOCK, BLOCK), 1)
+
+    def query_block(b):
+        halo_ready(b, (Q,))
+        featurize(conv(Q, b), qf, b)
+        scores = lax.dot_general(qf[b], kf[b], CONTRACT_LAST, preferred_element_type=F32)
+        scores = jnp.where(column_at <= row_at, scores, 0.0).astype(BF16)
+        loc[block_rows(b), :] = jnp.dot(
+            scores, vc[block_rows(b), :], preferred_element_type=F32
+        )
+
+    def query_step(i):
+        b = lax.rem(b0 + i, nb)
+        arrive_next(i, b, (Q,))
+        query_block(b)
+
     slices, slice_rows, slice_columns = chain_in.shape
     splits = m // slice_columns
     half = DH // 2
@@ -289,6 +306,10 @@
     def _():
         exclusive_pass()
 
+    ahead = jnp.maximum(z - 4, 0) + jnp.where(z == nz - 1, 2, 0)
+    arrive_first((Q,))
+    pl.loop(1, ahead + 1)(query_step)
+
     first.wait_recv()
     lower = (1 - core).astype(F32)
 
@@ -318,24 +339,6 @@
         other = tin[s].astype(F32)
         est[place(core, s)] = chain_in[s].astype(F32) + (1.0 - lower) * other
 
-    row_at = lax.broadcasted_iota(jnp.int32, (BLOCK, BLOCK), 0)
-    column_at = lax.broadcasted_iota(jnp.int32, (BLOCK, BLOCK), 1)
-
-    def query_block(b):
-        halo_ready(b, (Q,))
-        featurize(conv(Q, b), qf, b)
-        scores = lax.dot_general(qf[b], kf[b], CONTRACT_LAST, preferred_element_type=F32)
-        scores = jnp.where(column_at <= row_at, scores, 0.0).astype(BF16)
-        loc[block_rows(b), :] = jnp.dot(
-            scores, vc[block_rows(b), :], preferred_element_type=F32
-        )
-
-    def query_step(i):
-        b = lax.rem(b0 + i, nb)
-        arrive_next(i, b, (Q,))
-        query_block(b)
-
-    arrive_first((Q,))
     for s in range(slices):
         pair_copy(s, pair_out.at[s], pair_in.at[s]).wait_recv()
         est[place(1 - core, s)] = pair_in[s].astype(F32)
@@ -361,8 +364,11 @@
     @pl.loop(1, nb)
     def _(i):
         b = lax.rem(b0 + i, nb)
-        arrive_next(i, b, (Q,))
-        query_block(b)
+
+        @pl.when(i > ahead)
+        def _():
+            query_step(i)
+
         finish(b)
         for e in range(2):
             out_copy(2 * b + e).start()
@@ -452,15 +458,16 @@
                 dma((3,)),
             ],
             compiler_params=pltpu.CompilerParams(
-                collective_id=0, has_side_effects=True, vmem_limit_bytes=56 << 20
+                collective_id=0, has_side_effects=True, vmem_limit_bytes=52 << 20
             ),
         )(
             query_input,
             key_input,
             value_heads_input,
-            conv_weight,
-            feature_map,
-            out_gain.reshape(1, DH),
+            *(
+                pltpu.with_memory_space_constraint(w, pltpu.HBM)
+                for w in (conv_weight, feature_map, out_gain.reshape(1, DH))
+            ),
         )
 
     placed = (

time: 111 us -> 109 us (0.982)
  local copies, waits for them, and re-layouts: 2.29 us -> 0.97 us
    unnamed x1, local copies, waits for them, and re-layouts: 2.29 us -> 0.97 us
where the time goes in v3:
time: 109 us
  Pallas kernels  108 us (99%)
    pallas_call x1, Pallas kernels, local(): pl.pallas_call(functools.partial(kernel, nsp, ngrp), out_shape=jax.ShapeD...  108 us

profile of v3, /device:TPU:449, one launch (start us, length us, event | category | flops | bytes accessed | tf_op | source)
XLA Modules:
  0.0 108.6 jit_solution(8245709265715968248)
XLA Ops:
  0.0 107.6 %shard_map.64 = bf16[128,4096]{1,0:T(8,128)(2,1)S(1)} custom-call(bf16[128,4096]{1,0:T(8,128)(2,1)} %q_hbm.1, bf16[128,4096]{1,0:T(8,128)(2,1)} %k_hbm.1, bf16[128,4096]{1,0:T(8,128)(2,1)} %v_hbm.1, f32[3,4,128]{2,1,0:T(4,128)} %cw_hbm.1, bf16[128,1024]{1,0:T(8,128)(2,1)} %fm_hbm.1, f32[1,128]{1,0:T(1,128)} %bitcast.1), custom_call_target="tpu_custom_call" | custom-call | tf_op jit(solution)/shard_map/pallas_call | solution.py:421
  107.6 1.0 copy.8

commit v4 on v3

--- a/solution.py
+++ b/solution.py
@@ -306,7 +306,7 @@
     def _():
         exclusive_pass()
 
-    ahead = jnp.maximum(z - 4, 0) + jnp.where(z == nz - 1, 2, 0)
+    ahead = jnp.where(z == nz - 1, 2, 0)
     arrive_first((Q,))
     pl.loop(1, ahead + 1)(query_step)
 
@@ -338,6 +338,9 @@
     for s in range(slices):
         other = tin[s].astype(F32)
         est[place(core, s)] = chain_in[s].astype(F32) + (1.0 - lower) * other
+
+    done = ahead + 2
+    pl.loop(ahead + 1, done + 1)(query_step)
 
     for s in range(slices):
         pair_copy(s, pair_out.at[s], pair_in.at[s]).wait_recv()
@@ -365,7 +368,7 @@
     def _(i):
         b = lax.rem(b0 + i, nb)
 
-        @pl.when(i > ahead)
+        @pl.when(i > done)
         def _():
             query_step(i)
 

time: 109 us -> 109 us (level)
  no operation moved by 1% of the time
where the time goes in v4:
time: 109 us; the launch traced here: 108 us
  Pallas kernels  107 us (98%)
    pallas_call x1, Pallas kernels, local(): pl.pallas_call(functools.partial(kernel, nsp, ngrp), out_shape=jax.ShapeD...  107 us

profile of v4, /device:TPU:449, one launch (start us, length us, event | category | flops | bytes accessed | tf_op | source)
XLA Modules:
  0.0 108.3 jit_solution(8827396622585221572)
XLA Ops:
  0.0 107.3 %shard_map.64 = bf16[128,4096]{1,0:T(8,128)(2,1)S(1)} custom-call(bf16[128,4096]{1,0:T(8,128)(2,1)} %q_hbm.1, bf16[128,4096]{1,0:T(8,128)(2,1)} %k_hbm.1, bf16[128,4096]{1,0:T(8,128)(2,1)} %v_hbm.1, f32[3,4,128]{2,1,0:T(4,128)} %cw_hbm.1, bf16[128,1024]{1,0:T(8,128)(2,1)} %fm_hbm.1, f32[1,128]{1,0:T(1,128)} %bitcast.1), custom_call_target="tpu_custom_call" | custom-call | tf_op jit(solution)/shard_map/pallas_call | solution.py:424
  107.3 1.0 copy.8
